TPU v7x, 512 devices: a whole 4x4x16 slice. The times are simulated.
512 devices in a mesh: attn: 8 (over y, core), exp: 16 (over z), seq: 4 (over x).
Axes of the slice: x: 4, y: 4, z: 16, core: 2. Of those that a mesh axis runs over, the one named last changes fastest.
Arguments:
- tokens: bfloat16 [256, 6144], P(('attn', 'exp'), 'seq'), may hold values from -6 to 6
- modality: int32 [256], P(('attn', 'exp')), may hold values from 0 to 1, as said below
- cotangent: bfloat16 [256, 6144], P(('attn', 'exp'), 'seq'), may hold values from -6 to 6
- gate_speech: bfloat16 [6144, 24576], P('seq', ('attn', 'exp')), may hold values from -0.078125 to 0.078125
- up_speech: bfloat16 [6144, 24576], P('seq', ('attn', 'exp')), may hold values from -0.078125 to 0.078125
- down_speech: bfloat16 [24576, 6144], P(('attn', 'exp'), 'seq'), may hold values from -0.078125 to 0.078125
- gate_text: bfloat16 [6144, 16384], P('seq', ('attn', 'exp')), may hold values from -0.078125 to 0.078125
- up_text: bfloat16 [6144, 16384], P('seq', ('attn', 'exp')), may hold values from -0.078125 to 0.078125
- down_text: bfloat16 [16384, 6144], P(('attn', 'exp'), 'seq'), may hold values from -0.09375 to 0.09375
Outputs:
- mixed: bfloat16 [256, 6144], P(('attn', 'exp'), 'seq')
- token_grad: bfloat16 [256, 6144], P(('attn', 'exp'), 'seq')
- down_speech_grad: bfloat16 [24576, 6144], P(('attn', 'exp'), 'seq')
- down_text_grad: bfloat16 [16384, 6144], P(('attn', 'exp'), 'seq')
Inputs may be any that keep to these rules, and one draw needn't show every extreme that they name: Exactly 160 tokens of the window have modality 0 and the other 96 have modality 1, at places drawn from the seed.
All inputs are finite; a program needn't handle non-finite values.
Results may differ from a plain program's by a relative error of at most 0.005.
Values may be sent and summed in bfloat16 or wider, within the bound.
A program may use at most 64 MiB of HBM per device.

v0:
```python
import jax
import jax.numpy as jnp
from jax import lax
from jax.sharding import PartitionSpec as P


def contract_first(left, right):
    return lax.dot_general(
        left, right, (((0,), (0,)), ((), ())), preferred_element_type=jnp.float32
    )


def contract_last(left, right):
    return lax.dot_general(
        left, right, (((1,), (1,)), ((), ())), preferred_element_type=jnp.float32
    )


def shards(
    tokens, modality, cotangent, gate_speech, up_speech, down_speech, gate_text, up_text, down_text
):
    rows, grads, kinds = (
        lax.all_gather(tokens, ("attn", "exp"), axis=0, tiled=True),
        lax.all_gather(cotangent, ("attn", "exp"), axis=0, tiled=True),
        lax.all_gather(modality, ("attn", "exp"), axis=0, tiled=True),
    )
    speech = (kinds == 0)[:, None]
    features = lax.all_gather(rows, "seq", axis=1, tiled=True)
    full_gs, full_us, full_gt, full_ut = (
        lax.all_gather(gate_speech, "seq", axis=0, tiled=True),
        lax.all_gather(up_speech, "seq", axis=0, tiled=True),
        lax.all_gather(gate_text, "seq", axis=0, tiled=True),
        lax.all_gather(up_text, "seq", axis=0, tiled=True),
    )
    zero = jnp.zeros_like(grads)
    speech_grads = jnp.where(speech, grads, zero)
    text_grads = jnp.where(speech, zero, grads)
    terms = (
        jnp.dot(features, full_gs, preferred_element_type=jnp.float32),
        jnp.dot(features, full_us, preferred_element_type=jnp.float32),
        jnp.dot(features, full_gt, preferred_element_type=jnp.float32),
        jnp.dot(features, full_ut, preferred_element_type=jnp.float32),
    )
    gs, us, gt, ut = terms
    hs = (jax.nn.silu(gs) * us).astype(jnp.bfloat16)
    ht = (jax.nn.silu(gt) * ut).astype(jnp.bfloat16)
    speech_out = jnp.dot(hs, down_speech, preferred_element_type=jnp.float32)
    text_out = jnp.dot(ht, down_text, preferred_element_type=jnp.float32)
    partial_out = jnp.where(speech, speech_out, text_out)
    mixed = lax.psum_scatter(partial_out, ("attn", "exp"), scatter_dimension=0, tiled=True).astype(
        jnp.bfloat16
    )
    dhs, dht = lax.psum(
        (contract_last(speech_grads, down_speech), contract_last(text_grads, down_text)), "seq"
    )
    sig_s = jax.nn.sigmoid(gs)
    sig_t = jax.nn.sigmoid(gt)
    dgs = (dhs * us * sig_s * (1.0 + gs * (1.0 - sig_s))).astype(jnp.bfloat16)
    dus = (dhs * jax.nn.silu(gs)).astype(jnp.bfloat16)
    dgt = (dht * ut * sig_t * (1.0 + gt * (1.0 - sig_t))).astype(jnp.bfloat16)
    dut = (dht * jax.nn.silu(gt)).astype(jnp.bfloat16)
    speech_back = contract_last(dgs, gate_speech) + contract_last(dus, up_speech)
    text_back = contract_last(dgt, gate_text) + contract_last(dut, up_text)
    partial_grad = speech_back + text_back
    token_grad = lax.psum_scatter(
        partial_grad, ("attn", "exp"), scatter_dimension=0, tiled=True
    ).astype(jnp.bfloat16)
    down_speech_grad = contract_first(hs, speech_grads).astype(jnp.bfloat16)
    down_text_grad = contract_first(ht, text_grads).astype(jnp.bfloat16)
    return (mixed, token_grad, down_speech_grad, down_text_grad)


def solution(mesh):
    return jax.shard_map(
        shards,
        mesh=mesh,
        in_specs=(
            P(("attn", "exp"), "seq"),
            P(("attn", "exp")),
            P(("attn", "exp"), "seq"),
            P("seq", ("attn", "exp")),
            P("seq", ("attn", "exp")),
            P(("attn", "exp"), "seq"),
            P("seq", ("attn", "exp")),
            P("seq", ("attn", "exp")),
            P(("attn", "exp"), "seq"),
        ),
        out_specs=(
            P(("attn", "exp"), "seq"),
            P(("attn", "exp"), "seq"),
            P(("attn", "exp"), "seq"),
            P(("attn", "exp"), "seq"),
        ),
        check_vma=False,
    )
```

profile of v0, /device:TPU:2, one launch (start us, length us, event | category | flops | bytes accessed | tf_op | source)
XLA Modules:
  0.0 866.6 jit_solution(7845797920021915052)
XLA Ops:
  7.2 0.0 copy-start
  7.2 0.0 all-gather.10.cloned.1.call-start
  7.2 0.7 all-gather.10.cloned.1.call-update
  7.9 0.0 all-gather.8.cloned.1.call-start
  8.0 100.8 %all-gather = bf16[128,2,1536]{2,1,0:T(2,128)(2,1)S(1)} all-gather(bf16[1,2,1536]{2,1,0:T(2,128)(2,1)} %bitcast.24), channel_id=1, replica_groups=mesh['attn'=8,'exp'=16,'seq'=4] {'attn','exp'}, dimensions={0}, use_global_device_ids=true | all-gather | bytes 792576 | tf_op jit(solution)/shard_map/all_gather | solution.py:23
  108.8 1.2 reshape.13
  110.0 0.0 all-gather.8.cloned.1.call-update
  110.0 0.0 all-gather.12.cloned.1.call-start
  110.0 0.7 all-gather.12.cloned.1.call-update
  110.7 0.0 copy-start.15
  110.8 0.0 copy-start.16
  110.8 0.0 copy-start.13
  110.8 0.0 all-gather.14.cloned.1.call-start
  110.8 0.5 all-gather.14.cloned.1.call-update
  111.4 0.0 all-gather.16.cloned.1.call-start
  111.4 0.5 all-gather.16.cloned.1.call-update
  111.9 0.0 all-reduce.8.cloned.1.call-start
  112.0 0.0 copy-done.14
  112.0 92.1 %all-gather.1 = bf16[128,2,1536]{2,1,0:T(2,128)(2,1)S(1)} all-gather(bf16[1,2,1536]{2,1,0:T(2,128)(2,1)S(1)} %bitcast.25), channel_id=1, replica_groups=mesh['attn'=8,'exp'=16,'seq'=4] {'attn','exp'}, dimensions={0}, use_global_device_ids=true | all-gather | bytes 792576 | tf_op jit(solution)/shard_map/all_gather | solution.py:24
  204.1 0.3 reshape.15
  204.4 0.0 copy-start.9
  204.4 0.0 copy-done.15
  204.4 0.7 fusion.19
  205.8 0.0 copy-done.16
  205.8 0.2 dynamic-update-slice
  206.1 23.4 %all-reduce = s32[256]{0:T(256)S(1)} all-reduce(s32[256]{0:T(256)S(1)} %dynamic-update-slice), channel_id=1, replica_groups=mesh['attn'=8,'exp'=16,'seq'=4] {'attn','exp'}, use_global_device_ids=true, to_apply=%add | all-reduce | flops 256 | bytes 2048
  229.5 0.0 copy-done.13
  229.5 1.1 fusion.2
  230.6 0.0 copy-done
  230.6 1.2 fusion.1
  231.7 0.0 copy-done.9
  231.7 0.0 all-reduce.8.cloned.1.call-update
  232.4 0.0 all-gather.10.cloned.1.call-done
  232.4 0.0 all-gather.8.cloned.1.call-done
  232.5 3.8 fusion.20
  236.3 0.0 copy-start.4
  236.3 0.0 all-gather.12.cloned.1.call-done
  236.3 4.6 multiply_convert_fusion.2
  240.9 0.0 copy-done.4
  240.9 1.6 fusion.21
  242.4 3.3 fusion.22
  245.8 20.4 %all-gather.16.cloned.1.call-done = bf16[6144,128]{1,0:T(8,128)(2,1)} async-done(((bf16[1536,128]{1,0:T(8,128)(2,1)}), bf16[6144,128]{1,0:T(8,128)(2,1)}) %all-gather.16.cloned.1.call-update) | async-done | bytes 1572880 | tf_op jit(solution)/shard_map/all_gather | solution.py:33
  266.2 4.1 multiply_convert_fusion.5
  270.3 0.0 copy-done.1
  270.3 0.4 convolution_select_fusion
  270.6 0.8 copy-done.10
  271.4 1.1 convolution_convert_fusion.1
  272.5 1.2 convolution_convert_fusion
  273.7 52.4 %all-reduce.8.cloned.1.call-done = (f32[256,192]{0,1:T(8,128)}, f32[256,128]{1,0:T(8,128)}) async-done(((f32[256,192]{0,1:T(8,128)}, f32[256,128]{1,0:T(8,128)}), (f32[256,192]{0,1:T(8,128)}, f32[256,128]{1,0:T(8,128)})) %all-reduce.8.cloned.1.call-update) | async-done | bytes 327696 | tf_op jit(solution)/shard_map/psum | solution.py:53
  326.1 0.0 copy-done.2
  326.1 1.6 fusion.5
  327.7 0.0 copy-done.3
  327.7 0.0 copy-done.5
  327.7 0.0 copy-start.6
  327.8 0.4 convolution_add_fusion.1
  328.2 0.0 copy-start.7
  328.2 0.5 copy-done.6
  328.7 0.0 copy-done.11
  328.8 0.1 copy-done.12
  328.8 0.4 fusion.7
  329.2 0.0 copy-done.7
  329.3 1.6 fusion
  330.8 527.6 %all-reduce.9 = (bf16[256,1536]{1,0:T(8,128)(2,1)S(1)}, bf16[256,1536]{1,0:T(8,128)(2,1)}) all-reduce(f32[256,1536]{1,0:T(8,128)S(1)} %convolution_select_fusion, f32[256,1536]{1,0:T(8,128)} %fusion), channel_id=2, replica_groups=mesh['attn'=8,'exp'=16,'seq'=4] {'attn','exp'}, use_global_device_ids=true, to_apply=%region_0.1.clone | all-reduce | flops 786432 | bytes 4718592
  858.4 1.3 dynamic-slice_convert_fusion
  (13 shorter events, 0.0 us)
Async XLA Ops:
  7.2 223.4 %copy-start = (bf16[192,1536]{1,0:T(8,128)(2,1)S(1)}, bf16[192,1536]{1,0:T(8,128)(2,1)}, u32[]{:S(2)}) copy-start(bf16[192,1536]{1,0:T(8,128)(2,1)} %param.14) | copy-start | bytes 1769476
  7.2 225.3 %all-gather.10.cloned.1.call-start = ((), (), s32[]{:S(2)}) async-start(), calls=%async_computation.1 | async-start | bytes 2949120 | tf_op jit(solution)/shard_map/all_gather | solution.py:30
  7.9 224.5 %all-gather.8.cloned.1.call-start = ((), (), s32[]{:S(2)}) async-start(), calls=%async_computation | async-start | bytes 3932160 | tf_op jit(solution)/shard_map/all_gather | solution.py:28
  108.8 3.2 copy-start.14
  110.0 126.3 %all-gather.12.cloned.1.call-start = ((), (), s32[]{:S(2)}) async-start(), calls=%async_computation.2 | async-start | bytes 2949120 | tf_op jit(solution)/shard_map/all_gather | solution.py:31
  110.7 93.7 %copy-start.15 = (u32[512]{0:T(512)S(1)}, u32[512]{0:T(512)}, u32[]{:S(2)}) copy-start(u32[512]{0:T(512)} %constant.21) | copy-start | bytes 6148
  110.8 95.1 %copy-start.16 = (s32[2]{0:T(128)S(1)}, s32[2]{0:T(128)}, u32[]{:S(2)}) copy-start(s32[2]{0:T(128)} %param.10) | copy-start | bytes 28
  110.8 118.7 %copy-start.13 = (bf16[128,1536]{1,0:T(8,128)(2,1)S(1)}, bf16[128,1536]{1,0:T(8,128)(2,1)}, u32[]{:S(2)}) copy-start(bf16[128,1536]{1,0:T(8,128)(2,1)} %param.17) | copy-start | bytes 1179652
  110.8 131.7 %all-gather.14.cloned.1.call-start = ((), (), s32[]{:S(2)}) async-start(), calls=%async_computation.3 | async-start | bytes 1966080 | tf_op jit(solution)/shard_map/all_gather | solution.py:32
  111.4 154.8 %all-gather.16.cloned.1.call-start = ((), (), s32[]{:S(2)}) async-start(), calls=%async_computation.4 | async-start | bytes 1966080 | tf_op jit(solution)/shard_map/all_gather | solution.py:33
  111.9 214.2 %all-reduce.8.cloned.1.call-start = ((), (), s32[]{:S(2)}) async-start(), calls=%async_computation.5 | async-start | bytes 655360 | tf_op jit(solution)/shard_map/psum | solution.py:53
  204.4 27.3 %copy-start.9 = (bf16[256,1536]{1,0:T(8,128)(2,1)}, bf16[256,1536]{1,0:T(8,128)(2,1)S(1)}, u32[]{:S(2)}) copy-start(bf16[256,1536]{1,0:T(8,128)(2,1)S(1)} %reshape.15) | copy-start | bytes 2359300
  236.3 4.6 copy-start.4
  266.2 4.1 copy-start.1
  270.3 1.1 copy-start.10
  271.4 54.7 %copy-start.2 = (bf16[1536,192]{0,1:T(8,128)(2,1)S(1)}, bf16[1536,192]{0,1:T(8,128)(2,1)}, u32[]{:S(2)}) copy-start(bf16[1536,192]{0,1:T(8,128)(2,1)} %param.12) | copy-start | bytes 1769476
  273.7 54.0 %copy-start.3 = (bf16[1536,192]{0,1:T(8,128)(2,1)S(1)}, bf16[1536,192]{0,1:T(8,128)(2,1)}, u32[]{:S(2)}) copy-start(bf16[1536,192]{0,1:T(8,128)(2,1)} %param.13) | copy-start | bytes 1769476
  326.1 1.6 copy-start.5
  326.1 1.6 copy-start.8
  327.7 1.0 copy-start.6
  327.8 1.0 copy-start.11
  327.8 1.1 copy-start.12
  328.2 1.1 copy-start.7
Sparse Core Ops, SparseCore 0:
  10.1 44.2 all-gather.9
  110.1 40.5 all-gather.7
  152.8 40.8 all-gather.11
  195.6 34.1 all-gather.13
  231.8 34.3 all-gather.15
  268.4 57.6 all-reduce.7
where the time goes:
time: 867 us
  blocking collectives  744 us (86%)
  waiting for transfers between devices  75.3 us (9%)
  matrix products  26.2 us (3%)
  between operations  15.7 us (2%)
    unnamed x2, blocking collectives  551 us
    all_gather x1, blocking collectives, shards(): lax.all_gather(tokens, ('attn', 'exp'), axis=0, tiled=True)  101 us
    all_gather x1, blocking collectives, shards(): lax.all_gather(cotangent, ('attn', 'exp'), axis=0, tiled=True)  92.1 us
    psum x1, waiting for transfers between devices, shards(): lax.psum((contract_last(speech_grads, down_speech), contract_last(text_gr...  52.4 us
    all_gather x1, waiting for transfers between devices, shards(): lax.all_gather(up_text, 'seq', axis=0, tiled=True)  20.4 us
  transfers between devices with their start and end apart: 6, of which 2 were waited for; matrix products, arithmetic and copies ran while one was open for 3% of the time, Pallas kernels for 0%

commit v1 on v0

--- a/solution.py
+++ b/solution.py
@@ -20,7 +20,12 @@
     tokens, modality, cotangent, gate_speech, up_speech, down_speech, gate_text, up_text, down_text
 ):
     rows, grads, kinds = (
-        lax.all_gather(tokens, ("attn", "exp"), axis=0, tiled=True),
+        jnp.concatenate(
+            lax.all_to_all(
+                jnp.stack([tokens] * lax.axis_size(("attn", "exp"))), ("attn", "exp"), 0, 0
+            ),
+            axis=0,
+        ),
         lax.all_gather(cotangent, ("attn", "exp"), axis=0, tiled=True),
         lax.all_gather(modality, ("attn", "exp"), axis=0, tiled=True),
     )

time: 867 us -> 829 us (0.956)
  the two profiles are of different devices: /device:TPU:2 before, /device:TPU:6 now
where the time goes in v1:
time: 829 us; the launch traced here: 828 us
  blocking collectives  707 us (85%)
  waiting for transfers between devices  72.4 us (9%)
  matrix products  26.1 us (3%)
  between operations  15.7 us (2%)
    unnamed x2, blocking collectives  551 us
    all_gather x1, blocking collectives, shards(): lax.all_gather(cotangent, ('attn', 'exp'), axis=0, tiled=True)  94 us
    all_to_all x1, blocking collectives, shards(): lax.all_to_all(jnp.stack([tokens] * lax.axis_size(('attn', 'exp'))), ('at...  62.1 us
    psum x1, waiting for transfers between devices, shards(): lax.psum((contract_last(speech_grads, down_speech), contract_last(text_gr...  52.3 us
    all_gather x1, waiting for transfers between devices, shards(): lax.all_gather(up_text, 'seq', axis=0, tiled=True)  17.6 us
  transfers between devices with their start and end apart: 6, of which 2 were waited for; matrix products, arithmetic and copies ran while one was open for 3% of the time, Pallas kernels for 0%

profile of v1, /device:TPU:6, one launch (start us, length us, event | category | flops | bytes accessed | tf_op | source)
XLA Modules:
  0.0 828.2 jit_solution(17185344658421393670)
XLA Ops:
  7.2 0.0 copy-start
  7.2 0.0 all-gather.9.cloned.1.call-start
  7.2 0.7 all-gather.9.cloned.1.call-update
  7.9 0.0 all-gather.7.cloned.1.call-start
  8.0 1.1 stack.2
  9.1 62.1 %all_to_all.5 = bf16[128,2,1536]{2,1,0:T(2,128)(2,1)S(1)} all-to-all(bf16[128,2,1536]{2,1,0:T(2,128)(2,1)S(1)} %stack.2), channel_id=1, replica_groups=mesh['attn'=8,'exp'=16,'seq'=4] {'attn','exp'}, dimensions={0} | all-to-all | bytes 1572864 | tf_op jit(solution)/shard_map/all_to_all | solution.py:24
  71.2 1.2 reshape.14
  72.4 0.0 all-gather.7.cloned.1.call-update
  72.4 0.0 all-gather.11.cloned.1.call-start
  72.4 0.7 all-gather.11.cloned.1.call-update
  73.1 0.0 copy-start.15
  73.1 0.0 copy-start.16
  73.2 0.0 copy-start.13
  73.2 0.0 all-gather.13.cloned.1.call-start
  73.2 0.5 all-gather.13.cloned.1.call-update
  73.7 0.0 all-gather.15.cloned.1.call-start
  73.8 0.5 all-gather.15.cloned.1.call-update
  74.3 0.0 all-reduce.8.cloned.1.call-start
  74.4 0.0 copy-done.14
  74.4 94.0 %all-gather = bf16[128,2,1536]{2,1,0:T(2,128)(2,1)S(1)} all-gather(bf16[1,2,1536]{2,1,0:T(2,128)(2,1)S(1)} %bitcast.23), channel_id=1, replica_groups=mesh['attn'=8,'exp'=16,'seq'=4] {'attn','exp'}, dimensions={0}, use_global_device_ids=true | all-gather | bytes 792576 | tf_op jit(solution)/shard_map/all_gather | solution.py:29
  168.4 0.3 reshape.19
  168.7 0.0 copy-start.9
  168.7 0.0 copy-done.15
  168.7 0.7 fusion.19
  170.1 0.0 copy-done.16
  170.1 0.2 dynamic-update-slice
  170.4 23.5 %all-reduce = s32[256]{0:T(256)S(1)} all-reduce(s32[256]{0:T(256)S(1)} %dynamic-update-slice), channel_id=1, replica_groups=mesh['attn'=8,'exp'=16,'seq'=4] {'attn','exp'}, use_global_device_ids=true, to_apply=%add | all-reduce | flops 256 | bytes 2048
  193.8 0.0 copy-done.13
  193.8 1.1 fusion.2
  194.9 0.0 copy-done
  194.9 1.2 fusion.1
  196.1 0.0 copy-done.9
  196.1 0.0 all-reduce.8.cloned.1.call-update
  196.7 0.0 all-gather.9.cloned.1.call-done
  196.8 0.0 all-gather.7.cloned.1.call-done
  196.8 3.8 fusion.20
  200.6 0.0 copy-start.4
  200.6 0.0 all-gather.11.cloned.1.call-done
  200.6 4.6 multiply_convert_fusion.2
  205.2 0.0 copy-done.4
  205.2 1.6 fusion.21
  206.8 3.3 fusion.22
  210.1 17.6 %all-gather.15.cloned.1.call-done = bf16[6144,128]{1,0:T(8,128)(2,1)} async-done(((bf16[1536,128]{1,0:T(8,128)(2,1)}), bf16[6144,128]{1,0:T(8,128)(2,1)}) %all-gather.15.cloned.1.call-update) | async-done | bytes 1572880 | tf_op jit(solution)/shard_map/all_gather | solution.py:38
  227.7 4.1 multiply_convert_fusion.5
  231.8 0.3 convolution_select_fusion
  232.1 0.8 copy-done.10
  232.9 1.1 convolution_convert_fusion.1
  234.0 1.2 convolution_convert_fusion
  235.2 52.3 %all-reduce.8.cloned.1.call-done = (f32[256,192]{0,1:T(8,128)}, f32[256,128]{1,0:T(8,128)}) async-done(((f32[256,192]{0,1:T(8,128)}, f32[256,128]{1,0:T(8,128)}), (f32[256,192]{0,1:T(8,128)}, f32[256,128]{1,0:T(8,128)})) %all-reduce.8.cloned.1.call-update) | async-done | bytes 327696 | tf_op jit(solution)/shard_map/psum | solution.py:58
  287.5 1.6 fusion.5
  289.1 0.0 copy-done.3
  289.1 0.0 copy-done.5
  289.1 0.0 copy-done.8
  289.1 0.0 copy-start.6
  289.2 0.4 convolution_add_fusion.1
  289.6 0.0 copy-start.7
  289.6 0.5 copy-done.6
  290.1 0.0 copy-done.11
  290.2 0.1 copy-done.12
  290.2 0.4 fusion.7
  290.6 0.0 copy-done.7
  290.6 1.6 fusion
  292.2 527.8 %all-reduce.9 = (bf16[256,1536]{1,0:T(8,128)(2,1)S(1)}, bf16[256,1536]{1,0:T(8,128)(2,1)}) all-reduce(f32[256,1536]{1,0:T(8,128)S(1)} %convolution_select_fusion, f32[256,1536]{1,0:T(8,128)} %fusion), channel_id=2, replica_groups=mesh['attn'=8,'exp'=16,'seq'=4] {'attn','exp'}, use_global_device_ids=true, to_apply=%region_0.1.clone | all-reduce | flops 786432 | bytes 4718592
  820.0 1.3 dynamic-slice_convert_fusion
  (14 shorter events, 0.0 us)
Async XLA Ops:
  7.2 187.7 %copy-start = (bf16[192,1536]{1,0:T(8,128)(2,1)S(1)}, bf16[192,1536]{1,0:T(8,128)(2,1)}, u32[]{:S(2)}) copy-start(bf16[192,1536]{1,0:T(8,128)(2,1)} %param.14) | copy-start | bytes 1769476
  7.2 189.6 %all-gather.9.cloned.1.call-start = ((), (), s32[]{:S(2)}) async-start(), calls=%async_computation.2 | async-start | bytes 2949120 | tf_op jit(solution)/shard_map/all_gather | solution.py:35
  7.9 188.9 %all-gather.7.cloned.1.call-start = ((), (), s32[]{:S(2)}) async-start(), calls=%async_computation.1 | async-start | bytes 3932160 | tf_op jit(solution)/shard_map/all_gather | solution.py:33
  71.2 3.2 copy-start.14
  72.4 128.2 %all-gather.11.cloned.1.call-start = ((), (), s32[]{:S(2)}) async-start(), calls=%async_computation.3 | async-start | bytes 2949120 | tf_op jit(solution)/shard_map/all_gather | solution.py:36
  73.1 95.6 %copy-start.15 = (u32[512]{0:T(512)S(1)}, u32[512]{0:T(512)}, u32[]{:S(2)}) copy-start(u32[512]{0:T(512)} %constant.21) | copy-start | bytes 6148
  73.1 97.0 %copy-start.16 = (s32[2]{0:T(128)S(1)}, s32[2]{0:T(128)}, u32[]{:S(2)}) copy-start(s32[2]{0:T(128)} %param.10) | copy-start | bytes 28
  73.2 120.7 %copy-start.13 = (bf16[128,1536]{1,0:T(8,128)(2,1)S(1)}, bf16[128,1536]{1,0:T(8,128)(2,1)}, u32[]{:S(2)}) copy-start(bf16[128,1536]{1,0:T(8,128)(2,1)} %param.17) | copy-start | bytes 1179652
  73.2 133.6 %all-gather.13.cloned.1.call-start = ((), (), s32[]{:S(2)}) async-start(), calls=%async_computation.4 | async-start | bytes 1966080 | tf_op jit(solution)/shard_map/all_gather | solution.py:37
  73.7 153.9 %all-gather.15.cloned.1.call-start = ((), (), s32[]{:S(2)}) async-start(), calls=%async_computation.5 | async-start | bytes 1966080 | tf_op jit(solution)/shard_map/all_gather | solution.py:38
  74.3 213.2 %all-reduce.8.cloned.1.call-start = ((), (), s32[]{:S(2)}) async-start(), calls=%async_computation.6 | async-start | bytes 655360 | tf_op jit(solution)/shard_map/psum | solution.py:58
  168.7 27.3 %copy-start.9 = (bf16[256,1536]{1,0:T(8,128)(2,1)}, bf16[256,1536]{1,0:T(8,128)(2,1)S(1)}, u32[]{:S(2)}) copy-start(bf16[256,1536]{1,0:T(8,128)(2,1)S(1)} %reshape.19) | copy-start | bytes 2359300
  200.6 4.6 copy-start.4
  227.7 4.1 copy-start.1
  231.8 1.1 copy-start.10
  232.9 54.6 %copy-start.2 = (bf16[1536,192]{0,1:T(8,128)(2,1)S(1)}, bf16[1536,192]{0,1:T(8,128)(2,1)}, u32[]{:S(2)}) copy-start(bf16[1536,192]{0,1:T(8,128)(2,1)} %param.12) | copy-start | bytes 1769476
  235.2 53.9 %copy-start.3 = (bf16[1536,192]{0,1:T(8,128)(2,1)S(1)}, bf16[1536,192]{0,1:T(8,128)(2,1)}, u32[]{:S(2)}) copy-start(bf16[1536,192]{0,1:T(8,128)(2,1)} %param.13) | copy-start | bytes 1769476
  287.5 1.6 copy-start.5
  287.5 1.6 copy-start.8
  289.1 1.0 copy-start.6
  289.1 1.0 copy-start.11
  289.1 1.1 copy-start.12
  289.6 1.1 copy-start.7
Sparse Core Ops, SparseCore 0:
  10.1 43.2 all-gather.8
  72.5 38.6 all-gather.6
  113.3 40.9 all-gather.10
  156.2 35.1 all-gather.12
  193.3 34.3 all-gather.14
  229.9 57.5 all-reduce.7
